TPU v7x, 128 devices: a whole 4x4x4 slice. The times are simulated.
128 devices in a mesh: chan: 32 (over z_lo, y, x), seg: 4 (over z_hi, core).
Axes of the slice: x: 4, y: 4, z: 4 (z_hi: 2, z_lo: 2; z = z_hi * 2 + z_lo), core: 2. Of those that a mesh axis runs over, the one named last changes fastest.
Arguments:
- traces: bfloat16 [4096, 8, 8192], P('chan', 'seg'), may hold values from -20 to 20
- pair_offsets: int32 [32, 16], replicated, may hold values from 1 to 31, as said below
- pair_counts: int32 [32], replicated, may hold values from 1 to 16, 64 in all
- pair_owner: int32 [64], replicated, may hold values from 0 to 63, each once
Outputs:
- correlations: float32 [128, 64, 128, 256], P('seg', 'chan')
Inputs may be any that keep to these rules, and one draw needn't show every extreme that they name: `pair_offsets`: row a lists 16 distinct offsets; only its first pair_counts[a] entries name pairs. `pair_counts`: the counts sum to 64. `pair_owner`: every slot number appears once.
All inputs are finite; a program needn't handle non-finite values.
Results may differ from a plain program's by a relative error of at most 0.017.
Values may be sent and summed in bfloat16 or wider, within the bound.
No kernel may reach another device: no remote copies, remote signals or barrier semaphores. Data moves between devices by JAX's collectives and lax.ppermute only.
A program may use at most 128 MiB of HBM per device.

v0:
```python
import math
import jax
import jax.numpy as jnp
from jax import lax
from jax.sharding import PartitionSpec as P

SAMPLES = 8192
BAND_START = 32
FREQS = 512
HALF = 8
LAGS = 256
TILE_DEV = 2


def smoother(bin_count):
    bins_axis = lax.iota(jnp.int32, bin_count)
    nearby = (jnp.abs(bins_axis[:, None] - bins_axis[None, :]) <= HALF).astype(jnp.float32)
    return nearby / jnp.sum(nearby, axis=0, keepdims=True)


def lag_table(first_bin, bin_count):
    bins_axis = BAND_START + first_bin + lax.iota(jnp.int32, bin_count)
    shifts = jnp.mod(lax.iota(jnp.int32, LAGS) - LAGS // 2, SAMPLES)
    phase_index = jnp.mod(bins_axis[:, None] * shifts[None, :], SAMPLES)
    angles = phase_index.astype(jnp.float32) * (2.0 * math.pi / SAMPLES)
    return jnp.concatenate([jnp.cos(angles), -jnp.sin(angles)], axis=0).astype(jnp.bfloat16)


def pair_blocks(pair_offsets, pair_counts, pair_owner, block_count, slot_count):
    slot_index = lax.iota(jnp.int32, slot_count)
    starts = jnp.cumsum(pair_counts) - pair_counts
    first_block = jnp.sum((starts[None, :] <= slot_index[:, None]).astype(jnp.int32), axis=1) - 1
    member = lax.iota(jnp.int32, block_count)[None, :] == first_block[:, None]
    start_of = jnp.sum(jnp.where(member, starts[None, :], 0), axis=1)
    position = slot_index - start_of
    listed = jnp.sum(jnp.where(member[:, :, None], pair_offsets[None, :, :], 0), axis=1)
    chosen = lax.iota(jnp.int32, pair_offsets.shape[1])[None, :] == position[:, None]
    offset = jnp.sum(jnp.where(chosen, listed, 0), axis=1)
    second_block = jnp.mod(first_block + offset, block_count)
    held = pair_owner[None, :] == slot_index[:, None]
    slot_first = jnp.sum(jnp.where(held, first_block[None, :], 0), axis=1)
    slot_second = jnp.sum(jnp.where(held, second_block[None, :], 0), axis=1)
    return (slot_first, slot_second)


def cross_terms(first_spec, second_spec):
    turned = jnp.stack([first_spec[:, :, :, 1], -first_spec[:, :, :, 0]], axis=3)
    real_part = jnp.einsum(
        "tispf,tjspf->itjf", first_spec, second_spec, preferred_element_type=jnp.float32
    )
    imag_part = jnp.einsum(
        "tispf,tjspf->itjf", turned, second_spec, preferred_element_type=jnp.float32
    )
    return jnp.stack([real_part, imag_part], axis=3).astype(jnp.bfloat16)


def invert(spectra, table, norm_factor):
    flat = spectra.reshape(-1, spectra.shape[3] * spectra.shape[4])
    lagged = jnp.dot(flat, table, preferred_element_type=jnp.float32) * norm_factor
    return lagged.reshape(spectra.shape[:3] + (table.shape[1],))


def on_device(traces, pair_offsets, pair_counts, pair_owner):
    block_size, local_segs, sample_count = traces.shape
    parts_count = lax.axis_size("seg")
    block_count = lax.axis_size("chan")
    quarter_bins = FREQS // parts_count
    all_segs = local_segs * parts_count
    norm_factor = 1.0 / math.sqrt(FREQS * all_segs)
    signal = traces.reshape(block_size * local_segs, sample_count)
    width_bins = min(128, FREQS)
    pieces_count = FREQS // width_bins
    times_axis = lax.iota(jnp.int32, sample_count)

    def transform(piece_index):
        bins_axis = BAND_START + piece_index * width_bins + lax.iota(jnp.int32, width_bins)
        phase_index = jnp.mod(times_axis[:, None] * bins_axis[None, :], sample_count)
        angles = phase_index.astype(jnp.float32) * (2.0 * math.pi / sample_count)
        table_part = jnp.concatenate([jnp.cos(angles), -jnp.sin(angles)], axis=1)
        table_high = table_part.astype(jnp.bfloat16)
        table_low = (table_part - table_high.astype(jnp.float32)).astype(jnp.bfloat16)
        upper = jnp.dot(signal, table_high, preferred_element_type=jnp.float32)
        return upper + jnp.dot(signal, table_low, preferred_element_type=jnp.float32)

    spectrum = lax.map(transform, lax.iota(jnp.int32, pieces_count))
    spectrum = (
        spectrum.reshape(pieces_count, -1, 2, width_bins)
        .transpose(1, 2, 0, 3)
        .reshape(-1, 2, FREQS)
    )
    real_part = spectrum[:, 0]
    imag_part = spectrum[:, 1]
    amplitude = jnp.sqrt(real_part * real_part + imag_part * imag_part)
    smoothed = jnp.dot(
        amplitude,
        smoother(FREQS),
        precision=lax.Precision.HIGHEST,
        preferred_element_type=jnp.float32,
    )
    divisor = jnp.maximum(smoothed, 1.0)
    whitened = jnp.stack([real_part / divisor, imag_part / divisor], axis=1).astype(jnp.bfloat16)
    whitened = whitened.reshape(block_size, local_segs, 2, parts_count, quarter_bins)
    quarter = lax.all_to_all(whitened, "seg", split_axis=3, concat_axis=1, tiled=True)
    quarter = quarter.reshape(block_size, all_segs, 2, quarter_bins)
    slot_first, slot_second = pair_blocks(
        pair_offsets, pair_counts, pair_owner, block_count, TILE_DEV * block_count
    )
    my_start = lax.axis_index("chan") * TILE_DEV
    needed = jnp.concatenate(
        [
            lax.dynamic_slice_in_dim(slot_first, my_start, TILE_DEV),
            lax.dynamic_slice_in_dim(slot_second, my_start, TILE_DEV),
        ]
    )
    empty_blocks = jnp.zeros((2 * TILE_DEV, block_size, all_segs, 2, quarter_bins), jnp.bfloat16)
    incoming = lax.all_gather(quarter, "chan", axis=0, tiled=True)
    block_total = incoming.shape[0] // block_size
    incoming_blocks = incoming.reshape(block_total, block_size, all_segs, 2, quarter_bins)
    inside = (needed >= 0) & (needed < block_total)
    picked = jnp.take(incoming_blocks, jnp.clip(needed, 0, block_total - 1), axis=0)
    held_blocks = jnp.where(inside[:, None, None, None, None], picked, empty_blocks)
    first_spec = held_blocks[:TILE_DEV]
    second_spec = held_blocks[TILE_DEV:]
    full_table = lag_table(0, FREQS)
    spectra = cross_terms(first_spec, second_spec)
    return invert(
        lax.all_to_all(spectra, "seg", split_axis=0, concat_axis=4, tiled=True),
        full_table,
        norm_factor,
    )


def solution(mesh):
    placed = (P("chan", "seg", None), P(), P(), P())
    return jax.shard_map(
        on_device,
        mesh=mesh,
        in_specs=placed,
        out_specs=P("seg", "chan", None, None),
        check_vma=False,
    )
```

profile of v0, /device:TPU:1, one launch (start us, length us, event | category | flops | bytes accessed | tf_op | source)
XLA Modules:
  0.0 643.9 jit_solution(6079321119400441198)
XLA Ops:
  6.6 7.2 %reshape.215 = bf16[256,8192]{1,0:T(8,128)(2,1)} reshape(bf16[128,2,8192]{2,1,0:T(2,128)(2,1)} %param.6) | data formatting | bytes 8388608 | tf_op jit(solution)/shard_map/reshape | solution.py:70
  13.8 82.4 %while.13 = (s32[]{:T(128)}, f32[4,256,256]{1,2,0:T(8,128)S(1)}, s32[4]{0:T(128)S(1)}, bf16[256,8192]{1,0:T(8,128)(2,1)}, s32[]{:T(128)}, /*index=5*/s32[1]{0:T(128)}, s32[1]{0:T(128)}) while((s32[]{:T(128)}, f32[4,256,256]{1,2,0:T(8,128)S(1)}, s32[4]{0:T(128)S(1)}, bf16[256,8192]{1,0:T(8,128)(2,1)}, s32[]{:T(128)}, ...), condition=%wide.region_8.9_spmd.clone, body=%wide.region_7.8_spmd.clone.sunk | while | flops 2182152192 | bytes 51119252 | solution.py:85
  15.2 16.5 %fusion.57 = (f32[8192,128]{1,0:T(8,128)S(1)}, f32[8192,128]{1,0:T(8,128)S(1)}) fusion(s32[128]{0:T(128)S(1)} %iota_add_fusion.3), kind=kLoop, calls=%fused_computation.18.clone.1 | loop fusion | flops 15728640 | bytes 8389120 | tf_op jit(solution)/shard_map/while/body/eval_jaxpr/cos | solution.py:79
  33.0 1.3 fusion.59
  35.7 16.5 %fusion.57 = (f32[8192,128]{1,0:T(8,128)S(1)}, f32[8192,128]{1,0:T(8,128)S(1)}) fusion(s32[128]{0:T(128)S(1)} %iota_add_fusion.3), kind=kLoop, calls=%fused_computation.18.clone.1 | loop fusion | flops 15728640 | bytes 8389120 | tf_op jit(solution)/shard_map/while/body/eval_jaxpr/cos | solution.py:79
  53.6 1.3 fusion.59
  56.3 16.5 %fusion.57 = (f32[8192,128]{1,0:T(8,128)S(1)}, f32[8192,128]{1,0:T(8,128)S(1)}) fusion(s32[128]{0:T(128)S(1)} %iota_add_fusion.3), kind=kLoop, calls=%fused_computation.18.clone.1 | loop fusion | flops 15728640 | bytes 8389120 | tf_op jit(solution)/shard_map/while/body/eval_jaxpr/cos | solution.py:79
  74.1 1.3 fusion.59
  76.9 16.5 %fusion.57 = (f32[8192,128]{1,0:T(8,128)S(1)}, f32[8192,128]{1,0:T(8,128)S(1)}) fusion(s32[128]{0:T(128)S(1)} %iota_add_fusion.3), kind=kLoop, calls=%fused_computation.18.clone.1 | loop fusion | flops 15728640 | bytes 8389120 | tf_op jit(solution)/shard_map/while/body/eval_jaxpr/cos | solution.py:79
  98.6 15.9 %all_to_all.30 = bf16[128,2,2,4,128]{4,0,2,1,3:T(8,128)(2,1)} all-to-all(bf16[128,2,2,4,128]{4,0,2,1,3:T(8,128)(2,1)S(1)} %pad_maximum_fusion.2), channel_id=1, replica_groups=mesh['chan'=32,'seg'=4] {'seg'}, dimensions={3} | all-to-all | bytes 1048576 | tf_op jit(solution)/shard_map/all_to_all | solution.py:103
  115.8 186.4 %all-gather.2.cloned.1.call-done = bf16[4096,8,2,128]{3,0,2,1:T(8,128)(2,1)} async-done(((bf16[128,8,2,128]{3,0,2,1:T(8,128)(2,1)}), bf16[4096,8,2,128]{3,0,2,1:T(8,128)(2,1)}) %all-gather.2.cloned.1.call-update) | async-done | bytes 16777232 | tf_op jit(solution)/shard_map/all_gather | solution.py:116
  302.2 18.6 %copy.32 = bf16[4096,8,2,128]{3,1,2,0:T(8,128)(2,1)} copy(bf16[4096,8,2,128]{3,0,2,1:T(8,128)(2,1)} %all-gather.2.cloned.1.call-done) | data formatting | bytes 33554432 | tf_op jit(solution)/shard_map/all_gather | solution.py:116
  320.7 7.9 %gather_fusion = bf16[4,128,8,2,128]{4,2,3,1,0:T(8,128)(2,1)} fusion(bf16[32,128,8,2,128]{4,2,3,1,0:T(8,128)(2,1)} %bitcast.77, s32[1024]{0:T(1024)S(1)} %pad_clamp_fusion), kind=kCustom, calls=%fused_computation | custom fusion | bytes 4194320 | tf_op jit(solution)/shard_map/jit(_take)/gather | solution.py:120
  328.6 4.2 copy.33
  333.3 4.9 fusion.18
  338.2 4.9 fusion.19
  343.1 6.8 %pad_maximum_fusion.1 = bf16[128,2,128,2,128]{0,2,4,1,3:T(8,128)(2,1)} fusion(bf16[128,2,128,1,128]{0,2,4,1,3:T(8,128)(2,1)S(1)} %fusion.19, bf16[128,2,128,1,128]{0,2,4,1,3:T(8,128)(2,1)S(1)} %fusion.18), kind=kLoop, calls=%fused_computation.25 | loop fusion | flops 8388608 | bytes 33554432 | tf_op jit(solution)/shard_map/stack | solution.py:54
  349.9 23.5 %copy.34 = bf16[128,2,128,2,128]{2,4,1,3,0:T(8,128)(2,1)} copy(bf16[128,2,128,2,128]{0,2,4,1,3:T(8,128)(2,1)} %pad_maximum_fusion.1) | data formatting | bytes 33554432 | tf_op jit(solution)/shard_map/stack | solution.py:54
  373.4 12.9 %all-to-all-start.1 = ((bf16[128,2,128,2,128]{2,4,1,3,0:T(8,128)(2,1)}), bf16[128,2,128,2,128]{2,4,1,3,0:T(8,128)(2,1)}, u32[]{:S(2)}, u32[]{:S(2)}) async-start(bf16[128,2,128,2,128]{2,4,1,3,0:T(8,128)(2,1)} %copy.34), calls=%async_computation.1 | async-start | bytes 33554432 | tf_op jit(solution)/shard_map/all_to_all | solution.py:127
  386.3 2.5 cosine_convert_fusion
  388.8 181.2 %all-to-all-done.1 = bf16[128,2,128,2,128]{2,4,1,3,0:T(8,128)(2,1)} async-done(((bf16[128,2,128,2,128]{2,4,1,3,0:T(8,128)(2,1)}), bf16[128,2,128,2,128]{2,4,1,3,0:T(8,128)(2,1)}, u32[]{:S(2)}, u32[]{:S(2)}) %all-to-all-start.1) | async-done | bytes 16777248 | tf_op jit(solution)/shard_map/all_to_all | solution.py:127
  570.0 26.0 %copy.36 = bf16[32,2,128,2,4,128]{5,4,3,2,1,0:T(4,128)(2,1)} copy(bf16[32,2,128,2,4,128]{2,5,1,3,0,4:T(8,128)(2,1)} %bitcast.22) | data formatting | bytes 33554432 | tf_op jit(solution)/shard_map/all_to_all | solution.py:127
  596.0 27.3 %reshape.220 = bf16[8192,1024]{1,0:T(8,128)(2,1)} reshape(bf16[32,2,128,2,4,128]{5,4,3,2,1,0:T(4,128)(2,1)} %copy.36) | data formatting | bytes 33554432 | tf_op jit(solution)/shard_map/reshape | solution.py:58
  623.4 13.7 %convolution_multiply_fusion = f32[8192,256]{1,0:T(8,128)} fusion(bf16[8192,1024]{1,0:T(8,128)(2,1)} %reshape.220, bf16[512,256]{1,0:T(8,128)(2,1)S(1)} %get-tuple-element.99, bf16[512,256]{1,0:T(8,128)(2,1)S(1)} %get-tuple-element.98), kind=kOutput, calls=%fused_computation.28 | convolution fusion | flops 4298113024 | bytes 25690112 | tf_op jit(solution)/shard_map/dot_general | solution.py:59
  (65 shorter events, 13.4 us)
Async XLA Ops:
  6.5 295.6 %all-gather.2.cloned.1.call-start = ((), (), s32[]{:S(2)}) async-start(), calls=%async_computation.2 | async-start | bytes 17301504 | tf_op jit(solution)/shard_map/all_gather | solution.py:116
  15.2 16.5 %copy-start = (bf16[256,8192]{1,0:T(8,128)(2,1)S(1)}, bf16[256,8192]{1,0:T(8,128)(2,1)}, u32[]{:S(2)}) copy-start(bf16[256,8192]{1,0:T(8,128)(2,1)} %get-tuple-element.148) | copy-start | bytes 12582916 | tf_op jit(solution)/shard_map/while
  35.7 16.5 %copy-start = (bf16[256,8192]{1,0:T(8,128)(2,1)S(1)}, bf16[256,8192]{1,0:T(8,128)(2,1)}, u32[]{:S(2)}) copy-start(bf16[256,8192]{1,0:T(8,128)(2,1)} %get-tuple-element.148) | copy-start | bytes 12582916 | tf_op jit(solution)/shard_map/while
  56.3 16.5 %copy-start = (bf16[256,8192]{1,0:T(8,128)(2,1)S(1)}, bf16[256,8192]{1,0:T(8,128)(2,1)}, u32[]{:S(2)}) copy-start(bf16[256,8192]{1,0:T(8,128)(2,1)} %get-tuple-element.148) | copy-start | bytes 12582916 | tf_op jit(solution)/shard_map/while
  76.8 16.5 %copy-start = (bf16[256,8192]{1,0:T(8,128)(2,1)S(1)}, bf16[256,8192]{1,0:T(8,128)(2,1)}, u32[]{:S(2)}) copy-start(bf16[256,8192]{1,0:T(8,128)(2,1)} %get-tuple-element.148) | copy-start | bytes 12582916 | tf_op jit(solution)/shard_map/while
  98.2 16.2 %copy-start.2 = (s32[32]{0:T(128)S(1)}, s32[32]{0:T(128)}, u32[]{:S(2)}) copy-start(s32[32]{0:T(128)} %param.8) | copy-start | bytes 388
  98.2 16.5 %copy-start.1 = (s32[32,16]{0,1:T(8,128)S(1)}, s32[32,16]{0,1:T(8,128)}, u32[]{:S(2)}) copy-start(s32[32,16]{0,1:T(8,128)} %param.7) | copy-start | bytes 6148
  98.3 16.9 %copy-start.3 = (s32[64]{0:T(128)S(1)}, s32[64]{0:T(128)}, u32[]{:S(2)}) copy-start(s32[64]{0:T(128)} %param.9) | copy-start | bytes 772
  373.4 196.6 %all-to-all-start.1 = ((bf16[128,2,128,2,128]{2,4,1,3,0:T(8,128)(2,1)}), bf16[128,2,128,2,128]{2,4,1,3,0:T(8,128)(2,1)}, u32[]{:S(2)}, u32[]{:S(2)}) async-start(bf16[128,2,128,2,128]{2,4,1,3,0:T(8,128)(2,1)} %copy.34), calls=%async_computation.1 | async-start | bytes 33554432 | tf_op jit(solution)/shard_map/all_to_all | solution.py:127
Sparse Core Ops, SparseCore 0:
  114.6 187.5 all-gather.1
where the time goes:
time: 647 us; the launch traced here: 644 us
  waiting for transfers between devices  368 us (57%)
  local copies, waits for them, and re-layouts  119 us (18%)
  other arithmetic  76.8 us (12%)
  matrix products  35.1 us (5%)
  blocking collectives  15.9 us (2%)
  between operations  13.6 us (2%)
  starting transfers between devices  12.9 us (2%)
    all_gather x1, waiting for transfers between devices, on_device(): incoming = lax.all_gather(quarter, 'chan', axis=0, tiled=True)  186 us
    all_to_all x1, waiting for transfers between devices, on_device(): lax.all_to_all(spectra, 'seg', split_axis=0, concat_axis=4, tiled=True)  181 us
    cos x4, other arithmetic, transform(): table_part = jnp.concatenate([jnp.cos(angles), -jnp.sin(angles)], axis=1)  66.1 us
    reshape x1, local copies, waits for them, and re-layouts, invert(): flat = spectra.reshape(-1, spectra.shape[3] * spectra.shape[4])  27.3 us
    all_to_all x1, local copies, waits for them, and re-layouts, on_device(): lax.all_to_all(spectra, 'seg', split_axis=0, concat_axis=4, tiled=True)  26 us
    another operation x1, local copies, waits for them, and re-layouts, cross_terms(): return jnp.stack([real_part, imag_part], axis=3).astype(jnp.bfloat16)  23.5 us
    all_gather x1, local copies, waits for them, and re-layouts, on_device(): incoming = lax.all_gather(quarter, 'chan', axis=0, tiled=True)  18.6 us
    all_to_all x1, blocking collectives, on_device(): lax.all_to_all(whitened, 'seg', split_axis=3, concat_axis=1, tiled=True)  15.9 us
  transfers between devices with their start and end apart: 2, of which 2 were waited for; matrix products, arithmetic and copies ran while one was open for 1% of the time, Pallas kernels for 0%

commit v1 on v0

--- a/solution.py
+++ b/solution.py
@@ -100,7 +100,10 @@
     divisor = jnp.maximum(smoothed, 1.0)
     whitened = jnp.stack([real_part / divisor, imag_part / divisor], axis=1).astype(jnp.bfloat16)
     whitened = whitened.reshape(block_size, local_segs, 2, parts_count, quarter_bins)
-    quarter = lax.all_to_all(whitened, "seg", split_axis=3, concat_axis=1, tiled=True)
+    quarter = jnp.concatenate(
+        lax.all_to_all(jnp.stack(jnp.split(whitened, lax.axis_size("seg"), axis=3)), "seg", 0, 0),
+        axis=1,
+    )
     quarter = quarter.reshape(block_size, all_segs, 2, quarter_bins)
     slot_first, slot_second = pair_blocks(
         pair_offsets, pair_counts, pair_owner, block_count, TILE_DEV * block_count

time: 647 us -> 647 us (level)
  no operation moved by 1% of the time
where the time goes in v1:
time: 647 us; the launch traced here: 644 us
  waiting for transfers between devices  368 us (57%)
  local copies, waits for them, and re-layouts  119 us (18%)
  other arithmetic  76.8 us (12%)
  matrix products  35.1 us (5%)
  blocking collectives  15.9 us (2%)
  between operations  13.6 us (2%)
  starting transfers between devices  12.9 us (2%)
    all_gather x1, waiting for transfers between devices, on_device(): incoming = lax.all_gather(quarter, 'chan', axis=0, tiled=True)  186 us
    all_to_all x1, waiting for transfers between devices, on_device(): lax.all_to_all(spectra, 'seg', split_axis=0, concat_axis=4, tiled=True)  181 us
    cos x4, other arithmetic, transform(): table_part = jnp.concatenate([jnp.cos(angles), -jnp.sin(angles)], axis=1)  66.1 us
    reshape x1, local copies, waits for them, and re-layouts, invert(): flat = spectra.reshape(-1, spectra.shape[3] * spectra.shape[4])  27.3 us
    all_to_all x1, local copies, waits for them, and re-layouts, on_device(): lax.all_to_all(spectra, 'seg', split_axis=0, concat_axis=4, tiled=True)  26 us
    another operation x1, local copies, waits for them, and re-layouts, cross_terms(): return jnp.stack([real_part, imag_part], axis=3).astype(jnp.bfloat16)  23.5 us
    all_gather x1, local copies, waits for them, and re-layouts, on_device(): incoming = lax.all_gather(quarter, 'chan', axis=0, tiled=True)  18.6 us
    all_to_all x1, blocking collectives, on_device(): lax.all_to_all(jnp.stack(jnp.split(whitened, lax.axis_size('seg'), axis=3...  15.9 us
  transfers between devices with their start and end apart: 2, of which 2 were waited for; matrix products, arithmetic and copies ran while one was open for 1% of the time, Pallas kernels for 0%

profile of v1, /device:TPU:1, one launch (start us, length us, event | category | flops | bytes accessed | tf_op | source)
XLA Modules:
  0.0 644.0 jit_solution(6409358491178337120)
XLA Ops:
  6.6 7.2 %reshape.214 = bf16[256,8192]{1,0:T(8,128)(2,1)} reshape(bf16[128,2,8192]{2,1,0:T(2,128)(2,1)} %param.6) | data formatting | bytes 8388608 | tf_op jit(solution)/shard_map/reshape | solution.py:70
  13.8 82.4 %while.13 = (s32[]{:T(128)}, f32[4,256,256]{1,2,0:T(8,128)S(1)}, s32[4]{0:T(128)S(1)}, bf16[256,8192]{1,0:T(8,128)(2,1)}, s32[]{:T(128)}, /*index=5*/s32[1]{0:T(128)}, s32[1]{0:T(128)}) while((s32[]{:T(128)}, f32[4,256,256]{1,2,0:T(8,128)S(1)}, s32[4]{0:T(128)S(1)}, bf16[256,8192]{1,0:T(8,128)(2,1)}, s32[]{:T(128)}, ...), condition=%wide.region_8.9_spmd.clone, body=%wide.region_7.8_spmd.clone.sunk | while | flops 2182152192 | bytes 51119252 | solution.py:85
  15.2 16.5 %fusion.57 = (f32[8192,128]{1,0:T(8,128)S(1)}, f32[8192,128]{1,0:T(8,128)S(1)}) fusion(s32[128]{0:T(128)S(1)} %iota_add_fusion.3), kind=kLoop, calls=%fused_computation.18.clone.1 | loop fusion | flops 15728640 | bytes 8389120 | tf_op jit(solution)/shard_map/while/body/eval_jaxpr/cos | solution.py:79
  33.0 1.3 fusion.59
  35.7 16.5 %fusion.57 = (f32[8192,128]{1,0:T(8,128)S(1)}, f32[8192,128]{1,0:T(8,128)S(1)}) fusion(s32[128]{0:T(128)S(1)} %iota_add_fusion.3), kind=kLoop, calls=%fused_computation.18.clone.1 | loop fusion | flops 15728640 | bytes 8389120 | tf_op jit(solution)/shard_map/while/body/eval_jaxpr/cos | solution.py:79
  53.6 1.3 fusion.59
  56.3 16.5 %fusion.57 = (f32[8192,128]{1,0:T(8,128)S(1)}, f32[8192,128]{1,0:T(8,128)S(1)}) fusion(s32[128]{0:T(128)S(1)} %iota_add_fusion.3), kind=kLoop, calls=%fused_computation.18.clone.1 | loop fusion | flops 15728640 | bytes 8389120 | tf_op jit(solution)/shard_map/while/body/eval_jaxpr/cos | solution.py:79
  74.1 1.3 fusion.59
  76.9 16.5 %fusion.57 = (f32[8192,128]{1,0:T(8,128)S(1)}, f32[8192,128]{1,0:T(8,128)S(1)}) fusion(s32[128]{0:T(128)S(1)} %iota_add_fusion.3), kind=kLoop, calls=%fused_computation.18.clone.1 | loop fusion | flops 15728640 | bytes 8389120 | tf_op jit(solution)/shard_map/while/body/eval_jaxpr/cos | solution.py:79
  98.7 15.9 %all_to_all.20 = bf16[4,128,2,2,1,128]{5,1,4,3,2,0:T(8,128)(2,1)} all-to-all(bf16[4,128,2,2,1,128]{5,1,4,3,2,0:T(8,128)(2,1)S(1)} %pad_maximum_fusion.2), channel_id=1, replica_groups=mesh['chan'=32,'seg'=4] {'seg'}, dimensions={0} | all-to-all | bytes 1048576 | tf_op jit(solution)/shard_map/all_to_all | solution.py:104
  115.9 186.4 %all-gather.2.cloned.1.call-done = bf16[4096,8,2,128]{3,0,2,1:T(8,128)(2,1)} async-done(((bf16[128,8,2,128]{3,0,2,1:T(8,128)(2,1)}), bf16[4096,8,2,128]{3,0,2,1:T(8,128)(2,1)}) %all-gather.2.cloned.1.call-update) | async-done | bytes 16777232 | tf_op jit(solution)/shard_map/all_gather | solution.py:119
  302.3 18.6 %copy.41 = bf16[4096,8,2,128]{3,1,2,0:T(8,128)(2,1)} copy(bf16[4096,8,2,128]{3,0,2,1:T(8,128)(2,1)} %all-gather.2.cloned.1.call-done) | data formatting | bytes 33554432 | tf_op jit(solution)/shard_map/all_gather | solution.py:119
  320.8 7.9 %gather_fusion = bf16[4,128,8,2,128]{4,2,3,1,0:T(8,128)(2,1)} fusion(bf16[32,128,8,2,128]{4,2,3,1,0:T(8,128)(2,1)} %bitcast.87, s32[1024]{0:T(1024)S(1)} %pad_clamp_fusion), kind=kCustom, calls=%fused_computation | custom fusion | bytes 4194320 | tf_op jit(solution)/shard_map/jit(_take)/gather | solution.py:123
  328.7 4.2 copy.42
  333.4 4.9 fusion.18
  338.3 4.9 fusion.19
  343.2 6.8 %pad_maximum_fusion.1 = bf16[128,2,128,2,128]{0,2,4,1,3:T(8,128)(2,1)} fusion(bf16[128,2,128,1,128]{0,2,4,1,3:T(8,128)(2,1)S(1)} %fusion.19, bf16[128,2,128,1,128]{0,2,4,1,3:T(8,128)(2,1)S(1)} %fusion.18), kind=kLoop, calls=%fused_computation.25 | loop fusion | flops 8388608 | bytes 33554432 | tf_op jit(solution)/shard_map/stack | solution.py:54
  350.0 23.5 %copy.43 = bf16[128,2,128,2,128]{2,4,1,3,0:T(8,128)(2,1)} copy(bf16[128,2,128,2,128]{0,2,4,1,3:T(8,128)(2,1)} %pad_maximum_fusion.1) | data formatting | bytes 33554432 | tf_op jit(solution)/shard_map/stack | solution.py:54
  373.5 12.9 %all-to-all-start.1 = ((bf16[128,2,128,2,128]{2,4,1,3,0:T(8,128)(2,1)}), bf16[128,2,128,2,128]{2,4,1,3,0:T(8,128)(2,1)}, u32[]{:S(2)}, u32[]{:S(2)}) async-start(bf16[128,2,128,2,128]{2,4,1,3,0:T(8,128)(2,1)} %copy.43), calls=%async_computation.1 | async-start | bytes 33554432 | tf_op jit(solution)/shard_map/all_to_all | solution.py:130
  386.4 2.5 cosine_convert_fusion
  388.9 181.2 %all-to-all-done.1 = bf16[128,2,128,2,128]{2,4,1,3,0:T(8,128)(2,1)} async-done(((bf16[128,2,128,2,128]{2,4,1,3,0:T(8,128)(2,1)}), bf16[128,2,128,2,128]{2,4,1,3,0:T(8,128)(2,1)}, u32[]{:S(2)}, u32[]{:S(2)}) %all-to-all-start.1) | async-done | bytes 16777248 | tf_op jit(solution)/shard_map/all_to_all | solution.py:130
  570.1 26.0 %copy.45 = bf16[32,2,128,2,4,128]{5,4,3,2,1,0:T(4,128)(2,1)} copy(bf16[32,2,128,2,4,128]{2,5,1,3,0,4:T(8,128)(2,1)} %bitcast.27) | data formatting | bytes 33554432 | tf_op jit(solution)/shard_map/all_to_all | solution.py:130
  596.1 27.3 %reshape.219 = bf16[8192,1024]{1,0:T(8,128)(2,1)} reshape(bf16[32,2,128,2,4,128]{5,4,3,2,1,0:T(4,128)(2,1)} %copy.45) | data formatting | bytes 33554432 | tf_op jit(solution)/shard_map/reshape | solution.py:58
  623.4 13.7 %convolution_multiply_fusion = f32[8192,256]{1,0:T(8,128)} fusion(bf16[8192,1024]{1,0:T(8,128)(2,1)} %reshape.219, bf16[512,256]{1,0:T(8,128)(2,1)S(1)} %get-tuple-element.103, bf16[512,256]{1,0:T(8,128)(2,1)S(1)} %get-tuple-element.102), kind=kOutput, calls=%fused_computation.28 | convolution fusion | flops 4298113024 | bytes 25690112 | tf_op jit(solution)/shard_map/dot_general | solution.py:59
  (66 shorter events, 13.4 us)
Async XLA Ops:
  6.5 295.7 %all-gather.2.cloned.1.call-start = ((), (), s32[]{:S(2)}) async-start(), calls=%async_computation.2 | async-start | bytes 17301504 | tf_op jit(solution)/shard_map/all_gather | solution.py:119
  15.2 16.5 %copy-start = (bf16[256,8192]{1,0:T(8,128)(2,1)S(1)}, bf16[256,8192]{1,0:T(8,128)(2,1)}, u32[]{:S(2)}) copy-start(bf16[256,8192]{1,0:T(8,128)(2,1)} %get-tuple-element.152) | copy-start | bytes 12582916 | tf_op jit(solution)/shard_map/while
  35.7 16.5 %copy-start = (bf16[256,8192]{1,0:T(8,128)(2,1)S(1)}, bf16[256,8192]{1,0:T(8,128)(2,1)}, u32[]{:S(2)}) copy-start(bf16[256,8192]{1,0:T(8,128)(2,1)} %get-tuple-element.152) | copy-start | bytes 12582916 | tf_op jit(solution)/shard_map/while
  56.3 16.5 %copy-start = (bf16[256,8192]{1,0:T(8,128)(2,1)S(1)}, bf16[256,8192]{1,0:T(8,128)(2,1)}, u32[]{:S(2)}) copy-start(bf16[256,8192]{1,0:T(8,128)(2,1)} %get-tuple-element.152) | copy-start | bytes 12582916 | tf_op jit(solution)/shard_map/while
  76.8 16.5 %copy-start = (bf16[256,8192]{1,0:T(8,128)(2,1)S(1)}, bf16[256,8192]{1,0:T(8,128)(2,1)}, u32[]{:S(2)}) copy-start(bf16[256,8192]{1,0:T(8,128)(2,1)} %get-tuple-element.152) | copy-start | bytes 12582916 | tf_op jit(solution)/shard_map/while
  98.2 16.3 %copy-start.2 = (s32[32]{0:T(128)S(1)}, s32[32]{0:T(128)}, u32[]{:S(2)}) copy-start(s32[32]{0:T(128)} %param.8) | copy-start | bytes 388
  98.2 16.6 %copy-start.1 = (s32[32,16]{0,1:T(8,128)S(1)}, s32[32,16]{0,1:T(8,128)}, u32[]{:S(2)}) copy-start(s32[32,16]{0,1:T(8,128)} %param.7) | copy-start | bytes 6148
  98.3 17.0 %copy-start.3 = (s32[64]{0:T(128)S(1)}, s32[64]{0:T(128)}, u32[]{:S(2)}) copy-start(s32[64]{0:T(128)} %param.9) | copy-start | bytes 772
  373.5 196.6 %all-to-all-start.1 = ((bf16[128,2,128,2,128]{2,4,1,3,0:T(8,128)(2,1)}), bf16[128,2,128,2,128]{2,4,1,3,0:T(8,128)(2,1)}, u32[]{:S(2)}, u32[]{:S(2)}) async-start(bf16[128,2,128,2,128]{2,4,1,3,0:T(8,128)(2,1)} %copy.43), calls=%async_computation.1 | async-start | bytes 33554432 | tf_op jit(solution)/shard_map/all_to_all | solution.py:130
Sparse Core Ops, SparseCore 0:
  114.7 187.5 all-gather.1
